TPU v7x, 32 devices: a whole 2x2x4 slice. The times are simulated.
32 devices in a mesh: ctx: 8 (over z, x), head: 4 (over y, core).
Axes of the slice: x: 2, y: 2, z: 4, core: 2. Of those that a mesh axis runs over, the one named last changes fastest.
Arguments:
- positions: int32 [128], replicated, may hold values from 1 to 8191, as said below
- mla_queries: bfloat16 [128, 128, 576], P(None, 'head'), may hold values from -5000 to 5000
- latent_keys: bfloat16 [8192, 576], P('ctx'), may hold values from -18 to 18
- index_queries: bfloat16 [128, 64, 128], P(None, 'head'), may hold values from -64 to 64
- index_keys: bfloat16 [8192, 128], P('ctx'), may hold values from -18 to 18
- head_weights: float32 [128, 64], P(None, 'head'), may hold values from -4 to 4
Outputs:
- grad_queries: float32 [128, 64, 128], P('ctx', 'head')
- grad_keys: float32 [8192, 128], P(('ctx', 'head'))
- grad_weights: float32 [128, 64], P('ctx', 'head')
Inputs may be any that keep to these rules, and one draw needn't show every extreme that they name: Each query sees the keys at positions 0 to its own position.
All inputs are finite; a program needn't handle non-finite values.
Results may differ from a plain program's by a relative error of at most 0.0045.
Values may be sent and summed in bfloat16 or wider, within the bound.
A program may use at most 128 MiB of HBM per device.

v0:
```python
import math
import jax
import jax.numpy as jnp
from jax import lax
from jax.sharding import PartitionSpec as P

HEADS = 128
QK_HEAD = 192
masked_value = -1e30


def masked_highest(values, allowed):
    return jnp.max(jnp.where(allowed, values, masked_value), axis=-1)


def shifted_exp(values, allowed, highest):
    return jnp.where(allowed, jnp.exp(values - highest[..., None]), 0.0)


def local(positions, mla_queries, latent_keys, index_queries, index_keys, head_weights):
    rows = latent_keys.shape[0]
    key_pos = lax.axis_index("ctx") * rows + jnp.arange(rows, dtype=jnp.int32)
    allowed = key_pos[None, :] <= positions[:, None]
    scores = jnp.einsum(
        "thd,sd->hts", mla_queries, latent_keys, preferred_element_type=jnp.float32
    ) * (1.0 / math.sqrt(QK_HEAD))
    head_mask = allowed[None]
    highest = lax.pmax(masked_highest(scores, head_mask), "ctx")
    exponent = shifted_exp(scores, head_mask, highest)
    totals = lax.psum(jnp.sum(exponent, axis=-1), "ctx")
    factor = 1.0 / totals
    mla_part = jnp.sum(exponent * factor[..., None], axis=0)
    inner = jnp.einsum("tjd,sd->tjs", index_queries, index_keys, preferred_element_type=jnp.float32)
    active = jnp.maximum(inner, 0.0)
    logit_part = jnp.einsum("tj,tjs->ts", head_weights, active, precision=lax.Precision.HIGHEST)
    target, logits = (
        lax.psum_scatter(mla_part, "head", scatter_dimension=0, tiled=True),
        lax.psum_scatter(logit_part, "head", scatter_dimension=0, tiled=True),
    )
    share = target.shape[0]
    row_mask = lax.dynamic_slice_in_dim(allowed, lax.axis_index("head") * share, share, 0)
    target = target / HEADS
    index_high = lax.pmax(masked_highest(logits, row_mask), "ctx")
    index_exp = shifted_exp(logits, row_mask, index_high)
    index_sum = lax.psum(jnp.sum(index_exp, axis=-1), "ctx")
    index_factor = 1.0 / index_sum
    predicted = index_exp * index_factor[:, None]
    gradient = jnp.where(
        row_mask, math.sqrt(rows * lax.axis_size("ctx")) * (predicted - target), 0.0
    ).astype(jnp.bfloat16)
    gradient = lax.all_gather(gradient, "head", axis=0, tiled=True)
    grad_float = gradient.astype(jnp.float32)
    weight_part = jnp.einsum("ts,tjs->tj", grad_float, active, precision=lax.Precision.HIGHEST)
    delta = jnp.where(inner > 0, grad_float[:, None, :] * head_weights[:, :, None], 0.0).astype(
        jnp.bfloat16
    )
    query_part = jnp.einsum("tjs,sd->tjd", delta, index_keys, preferred_element_type=jnp.float32)
    grad_queries, grad_weights = (
        lax.psum_scatter(query_part, "ctx", scatter_dimension=0, tiled=True),
        lax.psum_scatter(weight_part, "ctx", scatter_dimension=0, tiled=True),
    )
    grad_keys = lax.psum_scatter(
        jnp.einsum("tjs,tjd->sd", delta, index_queries, preferred_element_type=jnp.float32),
        "head",
        scatter_dimension=0,
        tiled=True,
    )
    return (grad_queries, grad_keys, grad_weights)


def solution(mesh):
    in_specs = (
        P(),
        P(None, "head", None),
        P("ctx", None),
        P(None, "head", None),
        P("ctx", None),
        P(None, "head"),
    )
    out_specs = (P("ctx", "head", None), P(("ctx", "head"), None), P("ctx", "head"))
    return jax.shard_map(local, mesh=mesh, in_specs=in_specs, out_specs=out_specs, check_vma=False)
```

profile of v0, /device:TPU:0, one launch (start us, length us, event | category | flops | bytes accessed | tf_op | source)
XLA Modules:
  0.0 318.5 jit_solution(9850725890422266074)
XLA Ops:
  7.2 9.4 %broadcast_maximum_fusion = (f32[128,16,1024]{2,0,1:T(8,128)}, f32[128,1024]{1,0:T(8,128)}, f32[128,16,1024]{2,0,1:T(8,128)}) fusion(f32[128,16]{0,1:T(8,128)} %param.11, bf16[1024,128]{1,0:T(8,128)(2,1)} %param.10, bf16[128,16,128]{2,1,0:T(8,128)(2,1)} %param.9), kind=kOutput, calls=%fused_computation.24 | convolution fusion | flops 543031296 | bytes 18096128 | tf_op jit(solution)/shard_map/tjd,sd->tjs/dot_general | solution.py:33
  16.7 0.1 broadcast_compare_fusion
  16.9 0.3 copy.27
  17.1 13.1 %fusion = (f32[32,128]{1,0:T(8,128)S(1)}, f32[1024,128,32]{1,0,2:T(8,128)}) fusion(pred[128,1024]{0,1:T(8,128)(4,1)S(1)} %copy.27, bf16[128,32,576]{0,2,1:T(8,128)(2,1)} %param.7, bf16[1024,576]{0,1:T(8,128)(2,1)S(1)} %copy-done), kind=kOutput, calls=%fused_computation.2 | convolution fusion | flops 4844417024 | bytes 22822912 | tf_op jit(solution)/shard_map/thd,sd->hts/dot_general | solution.py:24
  30.3 10.9 %reduce-scatter.16.cloned.1.call-done = f32[32,1024]{1,0:T(8,128)} async-done(((f32[128,1024]{1,0:T(8,128)}), f32[32,1024]{1,0:T(8,128)}) %reduce-scatter.16.cloned.1.call-update) | async-done | bytes 131088 | tf_op jit(solution)/shard_map/reduce_scatter | solution.py:38
  41.2 1.0 select_reduce_fusion
  42.2 37.1 %all-reduce.1 = (f32[32,128]{1,0:T(8,128)S(1)}, f32[32]{0:T(128)S(1)}) all-reduce(f32[32,128]{1,0:T(8,128)S(1)} %get-tuple-element.21, f32[32]{0:T(128)S(1)} %select_reduce_fusion), channel_id=1, replica_groups=mesh['ctx'=8,'head'=4] {'ctx'}, use_global_device_ids=true, to_apply=%region_6.7 | all-reduce | flops 4128 | bytes 33024 | tf_op jit(solution)/shard_map/pmax | solution.py:28
  79.3 9.1 %fusion.3 = f32[32,128]{1,0:T(8,128)S(1)} fusion(f32[1024,128,32]{1,0,2:T(8,128)} %get-tuple-element.22, f32[32,128]{1,0:T(8,128)S(1)} %get-tuple-element.17, pred[128,1024]{0,1:T(8,128)(4,1)S(1)} %copy.27), kind=kLoop, calls=%fused_computation.6 | loop fusion | flops 16773120 | bytes 16941056 | tf_op jit(solution)/shard_map/reduce_sum | solution.py:30
  88.4 0.2 fusion.28
  88.6 33.0 %all-reduce = (f32[32,128]{1,0:T(8,128)S(1)}, f32[32]{0:T(128)S(1)}) all-reduce(f32[32,128]{1,0:T(8,128)S(1)} %fusion.3, f32[32]{0:T(128)S(1)} %fusion.28), channel_id=1, replica_groups=mesh['ctx'=8,'head'=4] {'ctx'}, use_global_device_ids=true, to_apply=%region_8.9 | all-reduce | flops 4128 | bytes 33024 | tf_op jit(solution)/shard_map/psum | solution.py:30
  121.7 8.0 %multiply_reduce_fusion = f32[128,1024]{0,1:T(8,128)S(1)} fusion(f32[1024,128,32]{1,0,2:T(8,128)} %get-tuple-element.22, f32[32,128]{1,0:T(8,128)S(1)} %broadcast_divide_fusion, f32[32,128]{1,0:T(8,128)S(1)} %get-tuple-element.17, pred[128,1024]{0,1:T(8,128)(4,1)S(1)} %copy.27), kind=kLoop, calls=%fused_computation.5 | loop fusion | flops 20840448 | bytes 17465344 | tf_op jit(solution)/shard_map/reduce_sum | solution.py:32
  129.7 1.0 copy.43
  130.7 0.2 reduce-scatter.10.cloned.1.call-start
  130.9 4.6 %fusion.8 = u16[128,1024]{1,0:T(8,128)(2,1)S(1)} fusion(f32[128,16,1024]{2,0,1:T(8,128)} %get-tuple-element.23), kind=kLoop, calls=%fused_computation.15 | loop fusion | flops 10354688 | bytes 8650752
  135.6 13.3 %reduce-scatter.18.cloned.1.call-done = f32[32,1024]{1,0:T(8,128)} async-done(((f32[128,1024]{1,0:T(8,128)}), f32[32,1024]{1,0:T(8,128)}) %reduce-scatter.18.cloned.1.call-update) | async-done | bytes 131088 | tf_op jit(solution)/shard_map/reduce_scatter | solution.py:37
  148.8 1.0 select_convert_fusion.5
  149.9 5.8 %all_gather.3 = bf16[128,1024]{1,0:T(8,128)(2,1)S(1)} all-gather(bf16[32,1024]{1,0:T(8,128)(2,1)S(1)} %select_convert_fusion.5), channel_id=1, replica_groups=mesh['ctx'=8,'head'=4] {'head'}, dimensions={0}, use_global_device_ids=true | all-gather | bytes 327680 | tf_op jit(solution)/shard_map/all_gather | solution.py:51
  155.7 2.4 fusion.7
  158.2 13.6 %fusion.4 = f32[128,1,16]{2,1,0:T(1,128)} fusion(f32[128,16,1024]{2,0,1:T(8,128)} %get-tuple-element.19, bf16[128,1024,1]{1,0,2:T(8,128)(2,1)S(1)} %bitcast.33), kind=kOutput, calls=%fused_computation.9 | convolution fusion | flops 25165824 | bytes 8658944 | tf_op jit(solution)/shard_map/ts,tjs->tj/dot_general | solution.py:53
  171.8 2.8 fusion.19
  174.7 48.2 %reduce-scatter.10.cloned.1.call-done = f32[16,16,128]{2,0,1:T(8,128)} async-done(((f32[128,16,128]{2,0,1:T(8,128)}), f32[16,16,128]{2,0,1:T(8,128)}) %reduce-scatter.10.cloned.1.call-update) | async-done | bytes 131088 | tf_op jit(solution)/shard_map/reduce_scatter | solution.py:59
  223.0 1.6 copy.31
  224.6 63.7 %reduce-scatter.14.cloned.1.call-done = f32[16,16]{1,0:T(8,128)} async-done(((f32[128,16]{1,0:T(8,128)}), f32[16,16]{1,0:T(8,128)}) %reduce-scatter.14.cloned.1.call-update) | async-done | bytes 1040 | tf_op jit(solution)/shard_map/reduce_scatter | solution.py:60
  288.2 23.7 %reduce-scatter.12.cloned.1.call-done = f32[256,128]{1,0:T(8,128)} async-done(((f32[1024,128]{1,0:T(8,128)}), f32[256,128]{1,0:T(8,128)}) %reduce-scatter.12.cloned.1.call-update) | async-done | bytes 131088 | tf_op jit(solution)/shard_map/reduce_scatter | solution.py:62
  (25 shorter events, 0.3 us)
Async XLA Ops:
  7.2 10.0 %copy-start = (bf16[1024,576]{0,1:T(8,128)(2,1)S(1)}, bf16[1024,576]{0,1:T(8,128)(2,1)}, u32[]{:S(2)}) copy-start(bf16[1024,576]{0,1:T(8,128)(2,1)} %param.8) | copy-start | bytes 3538948
  7.2 9.5 %copy-start.5 = (s32[128]{0:T(128)S(1)}, s32[128]{0:T(128)}, u32[]{:S(2)}) copy-start(s32[128]{0:T(128)} %param.6) | copy-start | bytes 1540
  7.2 34.0 %reduce-scatter.16.cloned.1.call-start = ((), (), s32[]{:S(2)}) async-start(), calls=%async_computation.8 | async-start | bytes 655360 | tf_op jit(solution)/shard_map/reduce_scatter | solution.py:38
  16.6 132.2 %reduce-scatter.18.cloned.1.call-start = ((), (), s32[]{:S(2)}) async-start(), calls=%async_computation.9 | async-start | bytes 655360 | tf_op jit(solution)/shard_map/reduce_scatter | solution.py:37
  79.3 9.1 %copy-start.1 = (f32[32,1024]{1,0:T(8,128)S(1)}, f32[32,1024]{1,0:T(8,128)}, u32[]{:S(2)}) copy-start(f32[32,1024]{1,0:T(8,128)} %reduce-scatter.16.cloned.1.call-done) | copy-start | bytes 393220
  129.7 26.0 %copy-start.3 = (bf16[1024,128]{1,0:T(8,128)(2,1)S(1)}, bf16[1024,128]{1,0:T(8,128)(2,1)}, u32[]{:S(2)}) copy-start(bf16[1024,128]{1,0:T(8,128)(2,1)} %param.10) | copy-start | bytes 786436
  129.7 26.0 %copy-start.4 = (f32[128,16]{0,1:T(8,128)S(1)}, f32[128,16]{0,1:T(8,128)}, u32[]{:S(2)}) copy-start(f32[128,16]{0,1:T(8,128)} %param.11) | copy-start | bytes 24580
  130.7 92.2 %reduce-scatter.10.cloned.1.call-start = ((), (), s32[]{:S(2)}) async-start(), calls=%async_computation.5 | async-start | bytes 1179648 | tf_op jit(solution)/shard_map/reduce_scatter | solution.py:59
  158.1 13.7 %copy-start.2 = (bf16[128,16,128]{2,1,0:T(8,128)(2,1)S(1)}, bf16[128,16,128]{2,1,0:T(8,128)(2,1)}, u32[]{:S(2)}) copy-start(bf16[128,16,128]{2,1,0:T(8,128)(2,1)} %param.9) | copy-start | bytes 1572868
  158.1 130.1 %reduce-scatter.14.cloned.1.call-start = ((), (), s32[]{:S(2)}) async-start(), calls=%async_computation.7 | async-start | bytes 73728 | tf_op jit(solution)/shard_map/reduce_scatter | solution.py:60
  171.8 140.2 %reduce-scatter.12.cloned.1.call-start = ((), (), s32[]{:S(2)}) async-start(), calls=%async_computation.6 | async-start | bytes 655360 | tf_op jit(solution)/shard_map/reduce_scatter | solution.py:62
Sparse Core Ops, SparseCore 0:
  16.8 24.3 reduce-scatter.15
  130.8 17.9 reduce-scatter.17
  158.2 64.6 reduce-scatter.9
  226.8 61.4 reduce-scatter.13
  291.2 20.7 reduce-scatter.11
where the time goes:
time: 319 us; the launch traced here: 318 us
  waiting for transfers between devices  160 us (50%)
  blocking collectives  75.9 us (24%)
  matrix products  41.3 us (13%)
  other arithmetic  24.2 us (8%)
  between operations  13.9 us (4%)
    reduce_scatter x1, waiting for transfers between devices, local(): lax.psum_scatter(weight_part, 'ctx', scatter_dimension=0, tiled=True)  63.7 us
    reduce_scatter x1, waiting for transfers between devices, local(): lax.psum_scatter(query_part, 'ctx', scatter_dimension=0, tiled=True)  48.2 us
    pmax x1, blocking collectives, local(): highest = lax.pmax(masked_highest(scores, head_mask), 'ctx')  37.1 us
    psum x1, blocking collectives, local(): totals = lax.psum(jnp.sum(exponent, axis=-1), 'ctx')  33 us
    reduce_scatter x1, waiting for transfers between devices, local(): lax.psum_scatter(jnp.einsum('tjs,tjd->sd', delta, index_queries, preferre...  23.7 us
    dot_general x1, matrix products, local(): jnp.einsum('ts,tjs->tj', grad_float, active, precision=lax.Precision.HIGH...  13.6 us
    reduce_scatter x1, waiting for transfers between devices, local(): lax.psum_scatter(mla_part, 'head', scatter_dimension=0, tiled=True)  13.3 us
    dot_general x1, matrix products, local(): jnp.einsum('thd,sd->hts', mla_queries, latent_keys, preferred_element_typ...  13.1 us
  transfers between devices with their start and end apart: 5, of which 5 were waited for; matrix products, arithmetic and copies ran while one was open for 11% of the time, Pallas kernels for 0%

commit v1 on v0

--- a/solution.py
+++ b/solution.py
@@ -27,7 +27,8 @@
     head_mask = allowed[None]
     highest = lax.pmax(masked_highest(scores, head_mask), "ctx")
     exponent = shifted_exp(scores, head_mask, highest)
-    totals = lax.psum(jnp.sum(exponent, axis=-1), "ctx")
+    t0 = jnp.sum(exponent, axis=-1)
+    totals = jnp.sum(lax.all_gather(t0, "ctx"), 0)
     factor = 1.0 / totals
     mla_part = jnp.sum(exponent * factor[..., None], axis=0)
     inner = jnp.einsum("tjd,sd->tjs", index_queries, index_keys, preferred_element_type=jnp.float32)

time: 319 us -> 318 us (level)
  waiting for transfers between devices: 160 us -> 144 us
  blocking collectives: 75.9 us -> 90.5 us
    all_gather x0 -> x1, blocking collectives: none -> 30.5 us  [local(): totals = jnp.sum(lax.all_gather(t0, 'ctx'), 0)]
    psum x1, blocking collectives: 33 us -> 17.1 us  [local(): index_sum = lax.psum(jnp.sum(index_exp, axis=-1), 'ctx')]
    reduce_scatter x1, waiting for transfers between devices: 13.3 us -> 0.01 us  [local(): lax.psum_scatter(mla_part, 'head', scatter_dimension=0, tiled=True)]
    reduce_sum x1 -> x2, other arithmetic: 9.14 us -> 9.12 us  [the longest x1 9.1 us: local(): t0 = jnp.sum(exponent, axis=-1)]
  transfers between devices with their start and end apart: 5 -> 5, of which waited for: 5 -> 4; matrix products, arithmetic and copies ran while one was open for 11% -> 11% of each run, Pallas kernels for 0% -> 0%
where the time goes in v1:
time: 318 us; the launch traced here: 317 us
  waiting for transfers between devices  144 us (45%)
  blocking collectives  90.5 us (28%)
  matrix products  41.3 us (13%)
  other arithmetic  24.2 us (8%)
  between operations  13.9 us (4%)
    reduce_scatter x1, waiting for transfers between devices, local(): lax.psum_scatter(weight_part, 'ctx', scatter_dimension=0, tiled=True)  63.7 us
    reduce_scatter x1, waiting for transfers between devices, local(): lax.psum_scatter(query_part, 'ctx', scatter_dimension=0, tiled=True)  45.9 us
    pmax x1, blocking collectives, local(): highest = lax.pmax(masked_highest(scores, head_mask), 'ctx')  37.1 us
    all_gather x1, blocking collectives, local(): totals = jnp.sum(lax.all_gather(t0, 'ctx'), 0)  30.5 us
    reduce_scatter x1, waiting for transfers between devices, local(): lax.psum_scatter(jnp.einsum('tjs,tjd->sd', delta, index_queries, preferre...  23.6 us
    psum x1, blocking collectives, local(): index_sum = lax.psum(jnp.sum(index_exp, axis=-1), 'ctx')  17.1 us
    dot_general x1, matrix products, local(): jnp.einsum('ts,tjs->tj', grad_float, active, precision=lax.Precision.HIGH...  13.6 us
    dot_general x1, matrix products, local(): jnp.einsum('thd,sd->hts', mla_queries, latent_keys, preferred_element_typ...  13.1 us
  transfers between devices with their start and end apart: 5, of which 4 were waited for; matrix products, arithmetic and copies ran while one was open for 11% of the time, Pallas kernels for 0%

profile of v1, /device:TPU:0, one launch (start us, length us, event | category | flops | bytes accessed | tf_op | source)
XLA Modules:
  0.0 317.5 jit_solution(14576498308140434938)
XLA Ops:
  7.2 9.4 %broadcast_maximum_fusion = (f32[128,16,1024]{2,0,1:T(8,128)}, f32[128,1024]{1,0:T(8,128)}, f32[128,16,1024]{2,0,1:T(8,128)}) fusion(f32[128,16]{0,1:T(8,128)} %param.11, bf16[1024,128]{1,0:T(8,128)(2,1)} %param.10, bf16[128,16,128]{2,1,0:T(8,128)(2,1)} %param.9), kind=kOutput, calls=%fused_computation.24 | convolution fusion | flops 543031296 | bytes 18096128 | tf_op jit(solution)/shard_map/tjd,sd->tjs/dot_general | solution.py:34
  16.7 0.1 broadcast_compare_fusion
  16.9 0.3 copy.32
  17.1 13.1 %fusion = (f32[32,128]{1,0:T(8,128)S(1)}, f32[1024,128,32]{1,0,2:T(8,128)}) fusion(pred[128,1024]{0,1:T(8,128)(4,1)S(1)} %copy.32, bf16[128,32,576]{0,2,1:T(8,128)(2,1)} %param.7, bf16[1024,576]{0,1:T(8,128)(2,1)S(1)} %copy-done), kind=kOutput, calls=%fused_computation.2 | convolution fusion | flops 4844417024 | bytes 22822912 | tf_op jit(solution)/shard_map/thd,sd->hts/dot_general | solution.py:24
  30.3 10.9 %reduce-scatter.16.cloned.1.call-done = f32[32,1024]{1,0:T(8,128)} async-done(((f32[128,1024]{1,0:T(8,128)}), f32[32,1024]{1,0:T(8,128)}) %reduce-scatter.16.cloned.1.call-update) | async-done | bytes 131088 | tf_op jit(solution)/shard_map/reduce_scatter | solution.py:39
  41.2 1.0 select_reduce_fusion
  42.2 37.1 %all-reduce = (f32[32,128]{1,0:T(8,128)S(1)}, f32[32]{0:T(128)S(1)}) all-reduce(f32[32,128]{1,0:T(8,128)S(1)} %get-tuple-element.22, f32[32]{0:T(128)S(1)} %select_reduce_fusion), channel_id=1, replica_groups=mesh['ctx'=8,'head'=4] {'ctx'}, use_global_device_ids=true, to_apply=%region_6.7 | all-reduce | flops 4128 | bytes 33024 | tf_op jit(solution)/shard_map/pmax | solution.py:28
  79.3 9.1 %fusion.3 = f32[32,128]{1,0:T(8,128)S(1)} fusion(f32[1024,128,32]{1,0,2:T(8,128)} %get-tuple-element.23, f32[32,128]{1,0:T(8,128)S(1)} %get-tuple-element.18, pred[128,1024]{0,1:T(8,128)(4,1)S(1)} %copy.32), kind=kLoop, calls=%fused_computation.6 | loop fusion | flops 16773120 | bytes 16941056 | tf_op jit(solution)/shard_map/reduce_sum | solution.py:30
  88.4 30.5 %all-gather = f32[256,128]{1,0:T(8,128)S(1)} all-gather(f32[32,128]{1,0:T(8,128)S(1)} %fusion.3), channel_id=2, replica_groups=mesh['ctx'=8,'head'=4] {'ctx'}, dimensions={0}, use_global_device_ids=true | all-gather | bytes 147456 | tf_op jit(solution)/shard_map/all_gather | solution.py:31
  118.9 8.0 %multiply_reduce_fusion = f32[128,1024]{0,1:T(8,128)S(1)} fusion(f32[1024,128,32]{1,0,2:T(8,128)} %get-tuple-element.23, f32[32,128]{1,0:T(8,128)S(1)} %broadcast_divide_fusion, f32[32,128]{1,0:T(8,128)S(1)} %get-tuple-element.18, pred[128,1024]{0,1:T(8,128)(4,1)S(1)} %copy.32), kind=kLoop, calls=%fused_computation.5 | loop fusion | flops 20840448 | bytes 17465344 | tf_op jit(solution)/shard_map/reduce_sum | solution.py:33
  127.0 1.0 copy.48
  128.0 0.2 reduce-scatter.10.cloned.1.call-start
  128.2 4.6 %fusion.8 = u16[128,1024]{1,0:T(8,128)(2,1)S(1)} fusion(f32[128,16,1024]{2,0,1:T(8,128)} %get-tuple-element.24), kind=kLoop, calls=%fused_computation.15 | loop fusion | flops 10354688 | bytes 8650752
  132.9 0.2 fusion.28
  133.1 17.1 %psum.7 = f32[32]{0:T(128)S(1)} all-reduce(f32[32]{0:T(128)S(1)} %fusion.28), channel_id=1, replica_groups=mesh['ctx'=8,'head'=4] {'ctx'}, use_global_device_ids=true, to_apply=%region_4.5 | all-reduce | flops 32 | bytes 256 | tf_op jit(solution)/shard_map/psum | solution.py:46
  150.2 1.0 select_convert_fusion.5
  151.2 5.8 %all_gather.11 = bf16[128,1024]{1,0:T(8,128)(2,1)S(1)} all-gather(bf16[32,1024]{1,0:T(8,128)(2,1)S(1)} %select_convert_fusion.5), channel_id=1, replica_groups=mesh['ctx'=8,'head'=4] {'head'}, dimensions={0}, use_global_device_ids=true | all-gather | bytes 327680 | tf_op jit(solution)/shard_map/all_gather | solution.py:52
  157.1 2.4 fusion.7
  159.5 13.6 %fusion.4 = f32[128,1,16]{2,1,0:T(1,128)} fusion(f32[128,16,1024]{2,0,1:T(8,128)} %get-tuple-element.20, bf16[128,1024,1]{1,0,2:T(8,128)(2,1)S(1)} %bitcast.34), kind=kOutput, calls=%fused_computation.9 | convolution fusion | flops 25165824 | bytes 8658944 | tf_op jit(solution)/shard_map/ts,tjs->tj/dot_general | solution.py:54
  173.2 2.8 fusion.19
  176.1 45.9 %reduce-scatter.10.cloned.1.call-done = f32[16,16,128]{2,0,1:T(8,128)} async-done(((f32[128,16,128]{2,0,1:T(8,128)}), f32[16,16,128]{2,0,1:T(8,128)}) %reduce-scatter.10.cloned.1.call-update) | async-done | bytes 131088 | tf_op jit(solution)/shard_map/reduce_scatter | solution.py:60
  222.0 1.6 copy.36
  223.6 63.7 %reduce-scatter.14.cloned.1.call-done = f32[16,16]{1,0:T(8,128)} async-done(((f32[128,16]{1,0:T(8,128)}), f32[16,16]{1,0:T(8,128)}) %reduce-scatter.14.cloned.1.call-update) | async-done | bytes 1040 | tf_op jit(solution)/shard_map/reduce_scatter | solution.py:61
  287.3 23.6 %reduce-scatter.12.cloned.1.call-done = f32[256,128]{1,0:T(8,128)} async-done(((f32[1024,128]{1,0:T(8,128)}), f32[256,128]{1,0:T(8,128)}) %reduce-scatter.12.cloned.1.call-update) | async-done | bytes 131088 | tf_op jit(solution)/shard_map/reduce_scatter | solution.py:63
  (27 shorter events, 0.4 us)
Async XLA Ops:
  7.2 10.0 %copy-start = (bf16[1024,576]{0,1:T(8,128)(2,1)S(1)}, bf16[1024,576]{0,1:T(8,128)(2,1)}, u32[]{:S(2)}) copy-start(bf16[1024,576]{0,1:T(8,128)(2,1)} %param.8) | copy-start | bytes 3538948
  7.2 9.5 %copy-start.5 = (s32[128]{0:T(128)S(1)}, s32[128]{0:T(128)}, u32[]{:S(2)}) copy-start(s32[128]{0:T(128)} %param.6) | copy-start | bytes 1540
  7.2 34.0 %reduce-scatter.16.cloned.1.call-start = ((), (), s32[]{:S(2)}) async-start(), calls=%async_computation.8 | async-start | bytes 655360 | tf_op jit(solution)/shard_map/reduce_scatter | solution.py:39
  16.6 133.6 %reduce-scatter.18.cloned.1.call-start = ((), (), s32[]{:S(2)}) async-start(), calls=%async_computation.9 | async-start | bytes 655360 | tf_op jit(solution)/shard_map/reduce_scatter | solution.py:38
  126.9 5.9 %copy-start.1 = (f32[32,1024]{1,0:T(8,128)S(1)}, f32[32,1024]{1,0:T(8,128)}, u32[]{:S(2)}) copy-start(f32[32,1024]{1,0:T(8,128)} %reduce-scatter.16.cloned.1.call-done) | copy-start | bytes 393220
  127.0 30.1 %copy-start.3 = (bf16[1024,128]{1,0:T(8,128)(2,1)S(1)}, bf16[1024,128]{1,0:T(8,128)(2,1)}, u32[]{:S(2)}) copy-start(bf16[1024,128]{1,0:T(8,128)(2,1)} %param.10) | copy-start | bytes 786436
  127.0 30.1 %copy-start.4 = (f32[128,16]{0,1:T(8,128)S(1)}, f32[128,16]{0,1:T(8,128)}, u32[]{:S(2)}) copy-start(f32[128,16]{0,1:T(8,128)} %param.11) | copy-start | bytes 24580
  128.0 94.0 %reduce-scatter.10.cloned.1.call-start = ((), (), s32[]{:S(2)}) async-start(), calls=%async_computation.5 | async-start | bytes 1179648 | tf_op jit(solution)/shard_map/reduce_scatter | solution.py:60
  159.5 13.7 %copy-start.2 = (bf16[128,16,128]{2,1,0:T(8,128)(2,1)S(1)}, bf16[128,16,128]{2,1,0:T(8,128)(2,1)}, u32[]{:S(2)}) copy-start(bf16[128,16,128]{2,1,0:T(8,128)(2,1)} %param.9) | copy-start | bytes 1572868
  159.5 127.8 %reduce-scatter.14.cloned.1.call-start = ((), (), s32[]{:S(2)}) async-start(), calls=%async_computation.7 | async-start | bytes 73728 | tf_op jit(solution)/shard_map/reduce_scatter | solution.py:61
  173.1 137.8 %reduce-scatter.12.cloned.1.call-start = ((), (), s32[]{:S(2)}) async-start(), calls=%async_computation.6 | async-start | bytes 655360 | tf_op jit(solution)/shard_map/reduce_scatter | solution.py:63
Sparse Core Ops, SparseCore 0:
  16.8 24.3 reduce-scatter.15
  128.1 17.9 reduce-scatter.17
  159.6 62.3 reduce-scatter.9
  225.8 61.4 reduce-scatter.13
  290.2 20.6 reduce-scatter.11
